TPU v7x, 32 devices: a whole 2x2x4 slice. The times are simulated.
32 devices in a mesh: dp: 4 (over y, x), ctx: 8 (over z, core).
Axes of the slice: x: 2, y: 2, z: 4, core: 2. Of those that a mesh axis runs over, the one named last changes fastest.
Arguments:
- inputs: float32 [4, 1024, 1088], P('dp', 'ctx'), may hold values from -6 to 6
- out_grad: float32 [4, 1024, 1088], P('dp', 'ctx'), may hold values from -6 to 6
- pair_blocks: int32 [8, 2], replicated, may hold values from 0 to 15, as said below
- triple_weight: float32 [1088, 3264], P('ctx', 'dp')
- merge_weight: float32 [1088, 1088], P('ctx', 'dp'), may hold values from -0.75 to 0.75
- expand_weight: float32 [1088, 4352], P('ctx', 'dp'), may hold values from -0.1875 to 0.1875
- shrink_weight: float32 [4352, 1088], P('ctx', 'dp'), may hold values from -0.09375 to 0.09375
- vector_params: float32 [1088, 12], P('ctx', 'dp')
- triple_moment: float32 [1088, 3264], P('ctx', 'dp'), may hold values from -24 to 24
- merge_moment: float32 [1088, 1088], P('ctx', 'dp'), may hold values from -6 to 6
- expand_moment: float32 [1088, 4352], P('ctx', 'dp'), may hold values from -6 to 6
- shrink_moment: float32 [4352, 1088], P('ctx', 'dp'), may hold values from -6 to 6
- vector_moment: float32 [1088, 12], P('ctx', 'dp'), may hold values from -112 to 112
- triple_square: float32 [1088, 3264], P('ctx', 'dp'), may hold values from 24.576 to 245.76
- merge_square: float32 [1088, 1088], P('ctx', 'dp'), may hold values from 8.192 to 81.92
- expand_square: float32 [1088, 4352], P('ctx', 'dp'), may hold values from 8.192 to 81.92
- shrink_square: float32 [4352, 1088], P('ctx', 'dp'), may hold values from 8.192 to 81.92
- vector_square: float32 [1088, 12], P('ctx', 'dp'), may hold values from 204.8 to 2048
Outputs:
- block_output: float32 [4, 1024, 1088], P('dp', 'ctx')
- input_grad: float32 [4, 1024, 1088], P('dp', 'ctx')
- triple_grad: float32 [1088, 3264], P('ctx', 'dp')
- merge_grad: float32 [1088, 1088], P('ctx', 'dp')
- expand_grad: float32 [1088, 4352], P('ctx', 'dp')
- shrink_grad: float32 [4352, 1088], P('ctx', 'dp')
- vector_grad: float32 [1088, 12], P('ctx', 'dp')
- triple_new: float32 [1088, 3264], P('ctx', 'dp')
- merge_new: float32 [1088, 1088], P('ctx', 'dp')
- expand_new: float32 [1088, 4352], P('ctx', 'dp')
- shrink_new: float32 [4352, 1088], P('ctx', 'dp')
- vector_new: float32 [1088, 12], P('ctx', 'dp')
- triple_moment_new: float32 [1088, 3264], P('ctx', 'dp')
- merge_moment_new: float32 [1088, 1088], P('ctx', 'dp')
- expand_moment_new: float32 [1088, 4352], P('ctx', 'dp')
- shrink_moment_new: float32 [4352, 1088], P('ctx', 'dp')
- vector_moment_new: float32 [1088, 12], P('ctx', 'dp')
- triple_square_new: float32 [1088, 3264], P('ctx', 'dp')
- merge_square_new: float32 [1088, 1088], P('ctx', 'dp')
- expand_square_new: float32 [1088, 4352], P('ctx', 'dp')
- shrink_square_new: float32 [4352, 1088], P('ctx', 'dp')
- vector_square_new: float32 [1088, 12], P('ctx', 'dp')
Inputs may be any that keep to these rules, and one draw needn't show every extreme that they name: `pair_blocks`: row c names the two blocks of 64 positions that stand in stored rows c * 2 * 64 onward: first a block p, then 2 * 8 - 1 - p; each of the 16 blocks is named once.
All inputs are finite; a program needn't handle non-finite values.
Results may differ from a plain program's by a relative error of at most 0.011.
Values may be sent and summed in bfloat16 or wider, within the bound.
A program may use at most 256 MiB of HBM per device.

v0:
```python
import jax
import jax.numpy as jnp
from jax import lax
from jax.sharding import PartitionSpec as P

D = 1088
H = 17
HD = 64
BLK = 64
norm_eps = 1e-05
beta_first = 0.9
beta_second = 0.95
learn_rate = 0.01
decay_rate = 0.1
adam_eps = 1e-08
adam_steps = 4
gelu_coef = 0.7978845608028654
masked_score = -1e30


def layer_norm(values):
    center = jnp.mean(values, axis=-1, keepdims=True)
    shifted = values - center
    inverse = lax.rsqrt(jnp.mean(shifted * shifted, axis=-1, keepdims=True) + norm_eps)
    return (shifted * inverse, inverse)


def norm_back(incoming, normed, inverse, gain_vec):
    scaled = incoming * gain_vec
    return inverse * (
        scaled
        - jnp.mean(scaled, axis=-1, keepdims=True)
        - normed * jnp.mean(scaled * normed, axis=-1, keepdims=True)
    )


def gelu_value(values):
    inside = gelu_coef * (values + 0.044715 * values * values * values)
    return 0.5 * values * (1.0 + jnp.tanh(inside))


def gelu_slope(values):
    inside = gelu_coef * (values + 0.044715 * values * values * values)
    tangent = jnp.tanh(inside)
    return 0.5 * (1.0 + tangent) + 0.5 * values * (1.0 - tangent * tangent) * gelu_coef * (
        1.0 + 3.0 * 0.044715 * values * values
    )


def adam_update(weight, gradient, moment, square, decayed):
    moment_new = beta_first * moment + (1.0 - beta_first) * gradient
    square_new = beta_second * square + (1.0 - beta_second) * gradient * gradient
    first_fix = 1.0 - beta_first**adam_steps
    second_fix = 1.0 - beta_second**adam_steps
    direction = moment_new / first_fix / (jnp.sqrt(square_new / second_fix) + adam_eps)
    if decayed:
        direction = direction + decay_rate * weight
    return (weight - learn_rate * direction, moment_new, square_new)


def split_heads(values):
    return values.reshape(values.shape[0], H, HD).transpose(1, 0, 2)


def join_heads(values):
    return values.transpose(1, 0, 2).reshape(values.shape[1], H * HD)


def gather_params(first_part, second_part, third_part, fourth_part, fifth_part):
    piece_one, piece_two, piece_three, piece_four, piece_five = (
        lax.all_gather(first_part, "ctx", axis=0, tiled=True),
        lax.all_gather(second_part, "ctx", axis=0, tiled=True),
        lax.all_gather(third_part, "ctx", axis=0, tiled=True),
        lax.all_gather(fourth_part, "ctx", axis=0, tiled=True),
        lax.all_gather(fifth_part, "ctx", axis=0, tiled=True),
    )
    return (
        lax.all_gather(piece_one, "dp", axis=1, tiled=True),
        lax.all_gather(piece_two, "dp", axis=1, tiled=True),
        lax.all_gather(piece_three, "dp", axis=1, tiled=True),
        lax.all_gather(piece_four, "dp", axis=1, tiled=True),
        lax.all_gather(piece_five, "dp", axis=1, tiled=True),
    )


def reduce_grads(first_part, second_part, third_part, fourth_part, fifth_part):
    piece_one, piece_two, piece_three, piece_four, piece_five = (
        lax.psum_scatter(first_part, "ctx", scatter_dimension=0, tiled=True),
        lax.psum_scatter(second_part, "ctx", scatter_dimension=0, tiled=True),
        lax.psum_scatter(third_part, "ctx", scatter_dimension=0, tiled=True),
        lax.psum_scatter(fourth_part, "ctx", scatter_dimension=0, tiled=True),
        lax.psum_scatter(fifth_part, "ctx", scatter_dimension=0, tiled=True),
    )
    return (
        lax.psum_scatter(piece_one, "dp", scatter_dimension=1, tiled=True),
        lax.psum_scatter(piece_two, "dp", scatter_dimension=1, tiled=True),
        lax.psum_scatter(piece_three, "dp", scatter_dimension=1, tiled=True),
        lax.psum_scatter(piece_four, "dp", scatter_dimension=1, tiled=True),
        lax.psum_scatter(piece_five, "dp", scatter_dimension=1, tiled=True),
    )


def gather_keys(key_rows, value_rows):
    return (
        lax.all_gather(key_rows, "ctx", axis=0, tiled=True),
        lax.all_gather(value_rows, "ctx", axis=0, tiled=True),
    )


def local(
    inputs,
    out_grad,
    pair_blocks,
    triple_weight,
    merge_weight,
    expand_weight,
    shrink_weight,
    vector_params,
    triple_moment,
    merge_moment,
    expand_moment,
    shrink_moment,
    vector_moment,
    triple_square,
    merge_square,
    expand_square,
    shrink_square,
    vector_square,
):
    rows_here = inputs.shape[1]
    stream = inputs[0]
    cotangent = out_grad[0]
    offsets = jnp.arange(BLK, dtype=jnp.int32)
    all_positions = (pair_blocks.reshape(-1)[:, None] * BLK + offsets[None, :]).reshape(-1)
    query_positions = lax.dynamic_slice_in_dim(
        all_positions, lax.axis_index("ctx") * rows_here, rows_here
    )
    allowed = query_positions[:, None] >= all_positions[None, :]
    score_scale = HD ** (-0.5)
    copy_triple = triple_weight.astype(jnp.bfloat16)
    copy_merge = merge_weight.astype(jnp.bfloat16)
    copy_expand = expand_weight.astype(jnp.bfloat16)
    copy_shrink = shrink_weight.astype(jnp.bfloat16)
    copy_vector = vector_params.astype(jnp.bfloat16)
    w_triple, w_merge, w_expand, w_shrink, w_vector = gather_params(
        copy_triple, copy_merge, copy_expand, copy_shrink, copy_vector
    )
    vectors = w_vector.astype(jnp.float32)
    gain_one = vectors[:, 0]
    shift_one = vectors[:, 1]
    query_bias = vectors[:, 2]
    value_bias = vectors[:, 3]
    merge_bias = vectors[:, 4]
    gain_two = vectors[:, 5]
    shift_two = vectors[:, 6]
    shrink_bias = vectors[:, 7]
    expand_bias = vectors[:, 8:12].T.reshape(-1)
    normed_one, inverse_one = layer_norm(stream)
    act_one = (normed_one * gain_one + shift_one).astype(jnp.bfloat16)
    triple = jnp.dot(act_one, w_triple, preferred_element_type=jnp.float32)
    query_b = (triple[:, :D] + query_bias).astype(jnp.bfloat16)
    key_b = triple[:, D : 2 * D].astype(jnp.bfloat16)
    value_b = (triple[:, 2 * D :] + value_bias).astype(jnp.bfloat16)
    keys_all, values_all = gather_keys(key_b, value_b)

    def head_scores(query_h, key_h):
        scores = (
            lax.dot_general(
                query_h, key_h, (((1,), (1,)), ((), ())), preferred_element_type=jnp.float32
            )
            * score_scale
        )
        return jnp.where(allowed, scores, masked_score)

    def head_forward(operands):
        query_h, key_h, value_h = operands
        scores = head_scores(query_h, key_h)
        row_max = jnp.max(scores, axis=1, keepdims=True)
        log_total = row_max + jnp.log(jnp.sum(jnp.exp(scores - row_max), axis=1, keepdims=True))
        probs_b = jnp.exp(scores - log_total).astype(jnp.bfloat16)
        attended = jnp.dot(probs_b, value_h, preferred_element_type=jnp.float32)
        return (attended.astype(jnp.bfloat16), log_total[:, 0])

    heads_query = split_heads(query_b)
    heads_key = split_heads(keys_all)
    heads_value = split_heads(values_all)
    heads_out, heads_total = lax.map(head_forward, (heads_query, heads_key, heads_value))
    attended_b = join_heads(heads_out)
    middle = stream + jnp.dot(attended_b, w_merge, preferred_element_type=jnp.float32) + merge_bias
    normed_two, inverse_two = layer_norm(middle)
    act_two = (normed_two * gain_two + shift_two).astype(jnp.bfloat16)
    pre_act = jnp.dot(act_two, w_expand, preferred_element_type=jnp.float32) + expand_bias
    hidden_b = gelu_value(pre_act).astype(jnp.bfloat16)
    block_out = (
        middle + jnp.dot(hidden_b, w_shrink, preferred_element_type=jnp.float32) + shrink_bias
    )
    back_triple, back_merge, back_expand, back_shrink, unused_vector = gather_params(
        copy_triple, copy_merge, copy_expand, copy_shrink, copy_vector
    )
    keys_again, values_again = gather_keys(key_b, value_b)
    back_key = split_heads(keys_again)
    back_value = split_heads(values_again)
    cotangent_b = cotangent.astype(jnp.bfloat16)
    shrink_local = jnp.dot(hidden_b.T, cotangent_b, preferred_element_type=jnp.float32)
    shrink_bias_grad = jnp.sum(cotangent, axis=0)
    dpre = jnp.dot(cotangent_b, back_shrink.T, preferred_element_type=jnp.float32) * gelu_slope(
        pre_act
    )
    dpre_b = dpre.astype(jnp.bfloat16)
    expand_local = jnp.dot(act_two.T, dpre_b, preferred_element_type=jnp.float32)
    expand_bias_grad = jnp.sum(dpre, axis=0)
    dact_two = jnp.dot(dpre_b, back_expand.T, preferred_element_type=jnp.float32)
    gain_two_grad = jnp.sum(dact_two * normed_two, axis=0)
    shift_two_grad = jnp.sum(dact_two, axis=0)
    dmiddle = cotangent + norm_back(dact_two, normed_two, inverse_two, gain_two)
    dmiddle_b = dmiddle.astype(jnp.bfloat16)
    merge_local = jnp.dot(attended_b.T, dmiddle_b, preferred_element_type=jnp.float32)
    merge_bias_grad = jnp.sum(dmiddle, axis=0)
    dattended_b = jnp.dot(dmiddle_b, back_merge.T, preferred_element_type=jnp.float32).astype(
        jnp.bfloat16
    )

    def head_backward(operands):
        query_h, key_h, value_h, out_h, dout_h, log_total = operands
        scores = head_scores(query_h, key_h)
        probs = jnp.exp(scores - log_total[:, None])
        probs_b = probs.astype(jnp.bfloat16)
        delta = jnp.sum(
            dout_h.astype(jnp.float32) * out_h.astype(jnp.float32), axis=1, keepdims=True
        )
        dprobs = lax.dot_general(
            dout_h, value_h, (((1,), (1,)), ((), ())), preferred_element_type=jnp.float32
        )
        dscores_b = (probs * (dprobs - delta) * score_scale).astype(jnp.bfloat16)
        dquery_h = jnp.dot(dscores_b, key_h, preferred_element_type=jnp.float32)
        dkey_h = lax.dot_general(
            dscores_b, query_h, (((0,), (0,)), ((), ())), preferred_element_type=jnp.float32
        )
        dvalue_h = lax.dot_general(
            probs_b, dout_h, (((0,), (0,)), ((), ())), preferred_element_type=jnp.float32
        )
        return (dquery_h, dkey_h, dvalue_h)

    dquery_heads, dkey_heads, dvalue_heads = lax.map(
        head_backward,
        (heads_query, back_key, back_value, heads_out, split_heads(dattended_b), heads_total),
    )
    dquery = join_heads(dquery_heads)
    dkey_rows, dvalue_rows = (
        lax.psum_scatter(join_heads(dkey_heads), "ctx", scatter_dimension=0, tiled=True),
        lax.psum_scatter(join_heads(dvalue_heads), "ctx", scatter_dimension=0, tiled=True),
    )
    dtriple_b = jnp.concatenate([dquery, dkey_rows, dvalue_rows], axis=1).astype(jnp.bfloat16)
    triple_local = jnp.dot(act_one.T, dtriple_b, preferred_element_type=jnp.float32)
    query_bias_grad = jnp.sum(dquery, axis=0)
    value_bias_grad = jnp.sum(dvalue_rows, axis=0)
    dact_one = jnp.dot(dtriple_b, back_triple.T, preferred_element_type=jnp.float32)
    gain_one_grad = jnp.sum(dact_one * normed_one, axis=0)
    shift_one_grad = jnp.sum(dact_one, axis=0)
    input_rows = dmiddle + norm_back(dact_one, normed_one, inverse_one, gain_one)
    vector_local = jnp.concatenate(
        [
            jnp.stack(
                [
                    gain_one_grad,
                    shift_one_grad,
                    query_bias_grad,
                    value_bias_grad,
                    merge_bias_grad,
                    gain_two_grad,
                    shift_two_grad,
                    shrink_bias_grad,
                ],
                axis=1,
            ),
            expand_bias_grad.reshape(4, D).T,
        ],
        axis=1,
    )
    triple_grad, merge_grad, expand_grad, shrink_grad, vector_grad = reduce_grads(
        triple_local, merge_local, expand_local, shrink_local, vector_local
    )
    triple_new, triple_moment_new, triple_square_new = adam_update(
        triple_weight, triple_grad, triple_moment, triple_square, True
    )
    merge_new, merge_moment_new, merge_square_new = adam_update(
        merge_weight, merge_grad, merge_moment, merge_square, True
    )
    expand_new, expand_moment_new, expand_square_new = adam_update(
        expand_weight, expand_grad, expand_moment, expand_square, True
    )
    shrink_new, shrink_moment_new, shrink_square_new = adam_update(
        shrink_weight, shrink_grad, shrink_moment, shrink_square, True
    )
    vector_new, vector_moment_new, vector_square_new = adam_update(
        vector_params, vector_grad, vector_moment, vector_square, False
    )
    return (
        block_out[None],
        input_rows[None],
        triple_grad,
        merge_grad,
        expand_grad,
        shrink_grad,
        vector_grad,
        triple_new,
        merge_new,
        expand_new,
        shrink_new,
        vector_new,
        triple_moment_new,
        merge_moment_new,
        expand_moment_new,
        shrink_moment_new,
        vector_moment_new,
        triple_square_new,
        merge_square_new,
        expand_square_new,
        shrink_square_new,
        vector_square_new,
    )


def solution(mesh):
    in_specs = (
        P("dp", "ctx", None),
        P("dp", "ctx", None),
        P(),
        P("ctx", "dp"),
        P("ctx", "dp"),
        P("ctx", "dp"),
        P("ctx", "dp"),
        P("ctx", "dp"),
        P("ctx", "dp"),
        P("ctx", "dp"),
        P("ctx", "dp"),
        P("ctx", "dp"),
        P("ctx", "dp"),
        P("ctx", "dp"),
        P("ctx", "dp"),
        P("ctx", "dp"),
        P("ctx", "dp"),
        P("ctx", "dp"),
    )
    out_specs = (
        P("dp", "ctx", None),
        P("dp", "ctx", None),
        P("ctx", "dp"),
        P("ctx", "dp"),
        P("ctx", "dp"),
        P("ctx", "dp"),
        P("ctx", "dp"),
        P("ctx", "dp"),
        P("ctx", "dp"),
        P("ctx", "dp"),
        P("ctx", "dp"),
        P("ctx", "dp"),
        P("ctx", "dp"),
        P("ctx", "dp"),
        P("ctx", "dp"),
        P("ctx", "dp"),
        P("ctx", "dp"),
        P("ctx", "dp"),
        P("ctx", "dp"),
        P("ctx", "dp"),
        P("ctx", "dp"),
        P("ctx", "dp"),
    )
    return jax.shard_map(local, mesh=mesh, in_specs=in_specs, out_specs=out_specs, check_vma=False)
```

profile of v0, /device:TPU:0, one launch (start us, length us, event | category | flops | bytes accessed | tf_op | source)
XLA Modules:
  0.0 1586.2 jit_solution(11072138455714467575)
XLA Ops:
  9.1 31.8 %all-gather.13.cloned.1.call-done = bf16[1088,816]{1,0:T(8,128)(2,1)} async-done(((bf16[136,816]{1,0:T(8,128)(2,1)}), bf16[1088,816]{1,0:T(8,128)(2,1)}) %all-gather.13.cloned.1.call-update) | async-done | bytes 1775632 | tf_op jit(solution)/shard_map/all_gather | solution.py:71
  40.9 4.0 copy.90
  46.9 12.8 all-gather
  59.8 8.8 all-gather.1
  69.6 55.4 %all-gather.15.cloned.1.call-done = bf16[1088,3264]{0,1:T(8,128)(2,1)} async-done(((bf16[1088,816]{0,1:T(8,128)(2,1)}), bf16[1088,3264]{0,1:T(8,128)(2,1)}) %all-gather.15.cloned.1.call-update) | async-done | bytes 7102480 | tf_op jit(solution)/shard_map/all_gather | solution.py:78
  125.0 5.4 fusion.75
  132.6 21.3 %all_gather.52 = bf16[1088,272]{1,0:T(8,128)(2,1)S(1)} all-gather(bf16[136,272]{1,0:T(8,128)(2,1)S(1)} %convert_element_type.74), channel_id=1, replica_groups=mesh['dp'=4,'ctx'=8] {'ctx'}, dimensions={0}, use_global_device_ids=true | all-gather | bytes 665856 | tf_op jit(solution)/shard_map/all_gather | solution.py:72
  155.0 11.0 all-gather.23.cloned.1.call-done
  166.0 5.1 copy.96
  173.4 28.5 %all-gather.29.cloned.1.call-done = bf16[8,544,272]{1,2,0:T(8,128)(2,1)} async-done(((bf16[1,544,272]{1,2,0:T(8,128)(2,1)}), bf16[8,544,272]{1,2,0:T(8,128)(2,1)}) %all-gather.29.cloned.1.call-update) | async-done | bytes 2367504 | tf_op jit(solution)/shard_map/all_gather | solution.py:74
  204.3 3.1 reshape.198
  208.6 26.0 %all-gather.17.cloned.1.call-done = bf16[1024,1088]{0,1:T(8,128)(2,1)} async-done(((bf16[128,1088]{0,1:T(8,128)(2,1)}), bf16[1024,1088]{0,1:T(8,128)(2,1)}) %all-gather.17.cloned.1.call-update) | async-done | bytes 2228240 | tf_op jit(solution)/shard_map/all_gather | solution.py:105
  234.7 5.2 copy.92
  239.9 27.4 %all-gather.19.cloned.1.call-done = bf16[1024,1088]{0,1:T(8,128)(2,1)} async-done(((bf16[128,1088]{0,1:T(8,128)(2,1)}), bf16[1024,1088]{0,1:T(8,128)(2,1)}) %all-gather.19.cloned.1.call-update) | async-done | bytes 2228240 | tf_op jit(solution)/shard_map/all_gather | solution.py:106
  267.3 5.3 copy.93
  272.6 69.9 %while.28 = (s32[]{:T(128)}, bf16[17,128,64]{1,2,0:T(8,128)(2,1)S(1)}, f32[17,128]{1,0:T(8,128)}, bf16[17,128,64]{2,1,0:T(8,128)(2,1)S(1)}, bf16[17,1024,64]{2,1...) while((s32[]{:T(128)}, ...), condition=%wide.region_5.6_spmd.clone, body=%wide.region_2.5_spmd.clone.sunk | while | flops 34611072 | bytes 2157681 | solution.py:187
  343.3 2.5 fusion.86
  346.6 63.8 %all-gather.25.cloned.1.call-done = bf16[1088,4352]{0,1:T(8,128)(2,1)} async-done(((bf16[1088,1088]{0,1:T(8,128)(2,1)}), bf16[1088,4352]{0,1:T(8,128)(2,1)}) %all-gather.25.cloned.1.call-update) | async-done | bytes 9469968 | tf_op jit(solution)/shard_map/all_gather | solution.py:80
  410.4 7.3 convolution_add_fusion
  417.6 91.1 %all-gather.27.cloned.1.call-done = bf16[4352,1088]{0,1:T(8,128)(2,1)} async-done(((bf16[4352,272]{0,1:T(8,128)(2,1)}), bf16[4352,1088]{0,1:T(8,128)(2,1)}) %all-gather.27.cloned.1.call-update) | async-done | bytes 9469968 | tf_op jit(solution)/shard_map/all_gather | solution.py:81
  508.8 7.5 fusion.87
  516.3 4.9 multiply_reduce_fusion
  523.8 133.4 %while.29 = (s32[]{:T(128)}, f32[17,128,64]{1,2,0:T(8,128)}, f32[17,1024,64]{1,2,0:T(8,128)}, f32[17,1024,64]{1,2,0:T(8,128)}, bf16[17,128,64]{2,1,0:T(8,128)(2,...) while((s32[]{:T(128)}, f32[17,128,64]{1,2,0:T(8,128)}, ...), condition=%wide.region_12.13_spmd.clone, body=%wide.region_10.12_spmd.clone.sunk | while | flops 85098368 | bytes 3944593 | solution.py:244
  658.1 3.0 fusion.69
  662.7 9.6 fusion.68
  674.2 35.6 %reduce-scatter.20.cloned.1.call-done = f32[128,1088]{0,1:T(8,128)} async-done(((f32[1024,1088]{0,1:T(8,128)}), f32[128,1088]{0,1:T(8,128)}) %reduce-scatter.20.cloned.1.call-update) | async-done | bytes 557072 | tf_op jit(solution)/shard_map/reduce_scatter | solution.py:250
  711.6 51.4 %reduce-scatter.22.cloned.1.call-done = f32[128,1088]{0,1:T(8,128)} async-done(((f32[1024,1088]{0,1:T(8,128)}), f32[128,1088]{0,1:T(8,128)}) %reduce-scatter.22.cloned.1.call-update) | async-done | bytes 557072 | tf_op jit(solution)/shard_map/reduce_scatter | solution.py:251
  765.8 8.5 fusion.65
  774.9 9.5 fusion.59
  784.5 37.1 %reduce-scatter.36.cloned.1.call-done = f32[136,1088]{1,0:T(8,128)} async-done(((f32[1088,1088]{1,0:T(8,128)}), f32[136,1088]{1,0:T(8,128)}) %reduce-scatter.36.cloned.1.call-update) | async-done | bytes 591888
  821.6 2.4 copy.110
  824.1 197.3 %reduce-scatter.28.cloned.1.call-done = f32[544,1088]{1,0:T(8,128)} async-done(((f32[4352,1088]{1,0:T(8,128)}), f32[544,1088]{1,0:T(8,128)}) %reduce-scatter.28.cloned.1.call-update) | async-done | bytes 2367504 | tf_op jit(solution)/shard_map/reduce_scatter | solution.py:91
  1021.5 147.7 %reduce-scatter.24.cloned.1.call-done = f32[136,3264]{1,0:T(8,128)} async-done(((f32[1088,3264]{1,0:T(8,128)}), f32[136,3264]{1,0:T(8,128)}) %reduce-scatter.24.cloned.1.call-update) | async-done | bytes 1775632 | tf_op jit(solution)/shard_map/reduce_scatter | solution.py:88
  1169.2 3.4 copy.108
  1172.7 186.2 %reduce-scatter.26.cloned.1.call-done = f32[136,4352]{1,0:T(8,128)} async-done(((f32[1088,4352]{1,0:T(8,128)}), f32[136,4352]{1,0:T(8,128)}) %reduce-scatter.26.cloned.1.call-update) | async-done | bytes 2367504 | tf_op jit(solution)/shard_map/reduce_scatter | solution.py:90
  1358.9 5.0 copy.112
  1370.5 2.4 copy.101
  1386.5 7.3 fusion.49
  1394.0 7.2 multiply_reduce_fusion.1
  1402.6 28.0 %all-reduce.2 = f32[1088,12]{0,1:T(8,128)} all-reduce(f32[1088,12]{0,1:T(8,128)} %concatenate.8), channel_id=12, replica_groups=mesh['dp'=4,'ctx'=8] {'ctx'}, use_global_device_ids=true, to_apply=%region_34.35.clone | all-reduce | flops 13056 | bytes 104448
  1432.0 17.5 %all-reduce.3 = f32[136,12]{0,1:T(8,128)} all-reduce(f32[136,12]{0,1:T(8,128)} %constant_dynamic-slice_fusion.2), channel_id=13, replica_groups=mesh['dp'=4,'ctx'=8] {'dp'}, use_global_device_ids=true, to_apply=%region_35.36.clone | all-reduce | flops 1632 | bytes 13056
  1457.1 11.4 all-reduce.6.cloned.1.call-done
  1468.5 3.9 multiply_subtract_fusion
  1472.4 2.4 copy.104
  1479.5 37.7 %reduce-scatter.30.cloned.1.call-done = f32[816,136]{1,0:T(8,128)} async-done(((f32[3264,136]{1,0:T(8,128)}), f32[816,136]{1,0:T(8,128)}) %reduce-scatter.30.cloned.1.call-update) | async-done | bytes 443920
  1518.6 2.7 multiply_subtract_fusion.2
  1521.3 53.7 %reduce-scatter.34.cloned.1.call-done = f32[1088,136]{1,0:T(8,128)} async-done(((f32[4352,136]{1,0:T(8,128)}), f32[1088,136]{1,0:T(8,128)}) %reduce-scatter.34.cloned.1.call-update) | async-done | bytes 591888
  1576.6 2.9 multiply_subtract_fusion.1
  (461 shorter events, 266.3 us)
Async XLA Ops:
  7.2 33.7 %all-gather.13.cloned.1.call-start = ((), (), s32[]{:S(2)}) async-start(), calls=%async_computation.9 | async-start | bytes 2193408 | tf_op jit(solution)/shard_map/all_gather | solution.py:71
  9.0 35.9 %copy-start.14 = (f32[136,1088]{1,0:T(8,128)S(1)}, f32[136,1088]{1,0:T(8,128)}, u32[]{:S(2)}) copy-start(f32[136,1088]{1,0:T(8,128)} %param.27) | copy-start | bytes 1775620
  9.0 116.0 %all-gather.15.cloned.1.call-start = ((), (), s32[]{:S(2)}) async-start(), calls=%async_computation.10 | async-start | bytes 9400320 | tf_op jit(solution)/shard_map/all_gather | solution.py:78
  44.9 23.7 %copy-start.1 = (f32[1,128,1088]{1,2,0:T(8,128)S(1)}, f32[1,128,1088]{1,2,0:T(8,128)}, u32[]{:S(2)}) copy-start(f32[1,128,1088]{1,2,0:T(8,128)} %param.22) | copy-start | bytes 1671172
  44.9 121.1 %all-gather.23.cloned.1.call-start = ((), (), s32[]{:S(2)}) async-start(), calls=%async_computation.14 | async-start | bytes 2820096 | tf_op jit(solution)/shard_map/all_gather | solution.py:73
  45.7 156.2 %all-gather.29.cloned.1.call-start = ((), (), s32[]{:S(2)}) async-start(), calls=%async_computation.22 | async-start | bytes 3133440 | tf_op jit(solution)/shard_map/all_gather | solution.py:74
  46.9 187.8 %all-gather.17.cloned.1.call-start = ((), (), s32[]{:S(2)}) async-start(), calls=%async_computation.11 | async-start | bytes 2506752 | tf_op jit(solution)/shard_map/all_gather | solution.py:105
  69.4 61.0 %copy-start.32 = (f32[1088]{0:T(1024)}, f32[1088]{0:T(1024)S(1)}, u32[]{:S(2)}) copy-start(f32[1088]{0:T(1024)S(1)} %get-tuple-element.323) | copy-start | bytes 13060
  69.4 61.0 %copy-start.34 = (f32[1088]{0:T(1024)}, f32[1088]{0:T(1024)S(1)}, u32[]{:S(2)}) copy-start(f32[1088]{0:T(1024)S(1)} %get-tuple-element.322) | copy-start | bytes 13060
  69.5 61.0 %copy-start.47 = (f32[128]{0:T(128)}, f32[128]{0:T(128)S(1)}, u32[]{:S(2)}) copy-start(f32[128]{0:T(128)S(1)} %broadcast_multiply_fusion.6) | copy-start | bytes 1540
  69.6 60.8 %copy-start.51 = (f32[128]{0:T(128)}, f32[128]{0:T(128)S(1)}, u32[]{:S(2)}) copy-start(f32[128]{0:T(128)S(1)} %add_rsqrt_fusion.1) | copy-start | bytes 1540
  131.2 136.1 %all-gather.19.cloned.1.call-start = ((), (), s32[]{:S(2)}) async-start(), calls=%async_computation.12 | async-start | bytes 2506752 | tf_op jit(solution)/shard_map/all_gather | solution.py:106
  132.5 210.1 %all-gather.21.cloned.1.call-start = ((), (), s32[]{:S(2)}) async-start(), calls=%async_computation.13 | async-start | bytes 3133440 | tf_op jit(solution)/shard_map/all_gather | solution.py:79
  155.0 255.4 %all-gather.25.cloned.1.call-start = ((), (), s32[]{:S(2)}) async-start(), calls=%async_computation.15 | async-start | bytes 12533760 | tf_op jit(solution)/shard_map/all_gather | solution.py:80
  171.2 337.6 %all-gather.27.cloned.1.call-start = ((), (), s32[]{:S(2)}) async-start(), calls=%async_computation.16 | async-start | bytes 11837440 | tf_op jit(solution)/shard_map/all_gather | solution.py:81
  207.4 502.4 %reduce-scatter.20.cloned.1.call-start = ((), (), s32[]{:S(2)}) async-start(), calls=%async_computation.17 | async-start | bytes 5013504 | tf_op jit(solution)/shard_map/reduce_scatter | solution.py:250
  272.6 70.7 %copy-start.37 = (f32[1088]{0:T(1024)S(1)}, f32[1088]{0:T(1024)}, u32[]{:S(2)}) copy-start(f32[1088]{0:T(1024)} %get-tuple-element.319) | copy-start | bytes 13060
  345.9 64.5 %copy-start.38 = (f32[128]{0:T(128)}, f32[128]{0:T(128)S(1)}, u32[]{:S(2)}) copy-start(f32[128]{0:T(128)S(1)} %broadcast_multiply_fusion.5) | copy-start | bytes 1540
  417.6 98.6 %copy-start.3 = (f32[128,4352]{1,0:T(8,128)}, f32[128,4352]{1,0:T(8,128)S(1)}, u32[]{:S(2)}) copy-start(f32[128,4352]{1,0:T(8,128)S(1)} %convolution_add_fusion) | copy-start | bytes 6684676
  508.7 7.5 copy-start
  508.7 7.5 copy-start.31
  508.7 7.5 copy-start.39
  508.7 7.5 copy-start.41
  522.2 135.8 %copy-start.5 = (f32[128,1088]{0,1:T(8,128)}, f32[128,1088]{0,1:T(8,128)S(1)}, u32[]{:S(2)}) copy-start(f32[128,1088]{0,1:T(8,128)S(1)} %get-tuple-element.382) | copy-start | bytes 1671172
  657.3 105.8 %reduce-scatter.22.cloned.1.call-start = ((), (), s32[]{:S(2)}) async-start(), calls=%async_computation.18 | async-start | bytes 5013504 | tf_op jit(solution)/shard_map/reduce_scatter | solution.py:251
  658.0 163.6 %reduce-scatter.36.cloned.1.call-start = ((), (), s32[]{:S(2)}) async-start(), calls=%async_computation.27 | async-start | bytes 5640192
  661.1 360.4 %reduce-scatter.28.cloned.1.call-start = ((), (), s32[]{:S(2)}) async-start(), calls=%async_computation.21 | async-start | bytes 22560768 | tf_op jit(solution)/shard_map/reduce_scatter | solution.py:91
  672.3 93.5 %copy-start.48 = (f32[128]{0:T(128)S(1)}, f32[128]{0:T(128)}, u32[]{:S(2)}) copy-start(f32[128]{0:T(128)} %copy-done.47) | copy-start | bytes 1540
  672.3 496.9 %reduce-scatter.24.cloned.1.call-start = ((), (), s32[]{:S(2)}) async-start(), calls=%async_computation.19 | async-start | bytes 16293888 | tf_op jit(solution)/shard_map/reduce_scatter | solution.py:88
  774.3 584.6 %reduce-scatter.26.cloned.1.call-start = ((), (), s32[]{:S(2)}) async-start(), calls=%async_computation.20 | async-start | bytes 21307392 | tf_op jit(solution)/shard_map/reduce_scatter | solution.py:90
  784.5 669.4 %reduce-scatter.32.cloned.1.call-start = ((), (), s32[]{:S(2)}) async-start(), calls=%async_computation.24 | async-start | bytes 1392640
  824.1 644.4 %all-reduce.6.cloned.1.call-start = ((), (), s32[]{:S(2)}) async-start(), calls=%async_computation.26 | async-start | bytes 5013504
  1021.5 495.7 %reduce-scatter.30.cloned.1.call-start = ((), (), s32[]{:S(2)}) async-start(), calls=%async_computation.23 | async-start | bytes 4177920
  1172.7 402.3 %reduce-scatter.34.cloned.1.call-start = ((), (), s32[]{:S(2)}) async-start(), calls=%async_computation.25 | async-start | bytes 5570560
  1363.9 11.5 copy-start.56
  1386.5 7.4 copy-start.25
  1386.5 7.4 copy-start.27
  1386.5 7.4 copy-start.33
  1386.5 7.4 copy-start.49
  1386.5 7.4 copy-start.52
  1394.0 58.2 %copy-start.6 = (f32[128,1088]{0,1:T(8,128)S(1)}, f32[128,1088]{0,1:T(8,128)}, u32[]{:S(2)}) copy-start(f32[128,1088]{0,1:T(8,128)} %copy-done.5) | copy-start | bytes 1671172
  1402.6 66.0 %copy-start.9 = (f32[544,272]{1,0:T(8,128)S(1)}, f32[544,272]{1,0:T(8,128)}, u32[]{:S(2)}) copy-start(f32[544,272]{1,0:T(8,128)} %copy.103) | copy-start | bytes 1775620
  1402.6 66.0 %copy-start.10 = (f32[544,272]{1,0:T(8,128)S(1)}, f32[544,272]{1,0:T(8,128)}, u32[]{:S(2)}) copy-start(f32[544,272]{1,0:T(8,128)} %copy.100) | copy-start | bytes 1775620
  1455.0 17.4 %copy-start.29 = (f32[136,272]{1,0:T(8,128)}, f32[136,272]{1,0:T(8,128)S(1)}, u32[]{:S(2)}) copy-start(f32[136,272]{1,0:T(8,128)S(1)} %copy.111) | copy-start | bytes 443908
  1477.1 41.4 %copy-start.18 = (f32[136,816]{1,0:T(8,128)S(1)}, f32[136,816]{1,0:T(8,128)}, u32[]{:S(2)}) copy-start(f32[136,816]{1,0:T(8,128)} %param.25) | copy-start | bytes 1331716
  1518.6 58.0 %copy-start.17 = (f32[136,816]{1,0:T(8,128)}, f32[136,816]{1,0:T(8,128)S(1)}, u32[]{:S(2)}) copy-start(f32[136,816]{1,0:T(8,128)S(1)} %copy.109) | copy-start | bytes 1331716
  1518.6 58.0 %copy-start.15 = (f32[136,1088]{1,0:T(8,128)S(1)}, f32[136,1088]{1,0:T(8,128)}, u32[]{:S(2)}) copy-start(f32[136,1088]{1,0:T(8,128)} %param.27) | copy-start | bytes 1775620
  1518.6 58.0 %copy-start.30 = (f32[136,1088]{1,0:T(8,128)S(1)}, f32[136,1088]{1,0:T(8,128)}, u32[]{:S(2)}) copy-start(f32[136,1088]{1,0:T(8,128)} %param.32) | copy-start | bytes 1775620
  (28 other events, 115.5 us)
Sparse Core Ops, SparseCore 0:
  10.2 30.6 all-gather.12
  45.0 79.9 all-gather.14
  127.2 38.7 all-gather.22
  168.1 33.8 all-gather.28
  203.9 30.6 all-gather.16
  236.7 30.5 all-gather.18
  269.7 37.5 all-gather.20
  309.2 101.1 all-gather.24
  412.2 96.4 all-gather.26
  657.4 52.3 reduce-scatter.19
  712.1 50.8 reduce-scatter.21
  765.2 56.3 reduce-scatter.35
  824.0 197.4 reduce-scatter.27
  1023.6 145.5 reduce-scatter.23
  1171.4 187.4 reduce-scatter.25
  1361.7 26.8 reduce-scatter.31
  1391.6 76.8 all-reduce.5
  1471.4 45.6 reduce-scatter.29
  1520.2 54.7 reduce-scatter.33
where the time goes:
time: 1600 us; the launch traced here: 1590 us
  waiting for transfers between devices  1090 us (68%)
  matrix products  234 us (15%)
  local copies, waits for them, and re-layouts  113 us (7%)
  blocking collectives  88.3 us (6%)
  other arithmetic  38.1 us (2%)
  between operations  16.8 us (1%)
    reduce_scatter x1, waiting for transfers between devices, reduce_grads(): lax.psum_scatter(fourth_part, 'ctx', scatter_dimension=0, tiled=True)  197 us
    reduce_scatter x1, waiting for transfers between devices, reduce_grads(): lax.psum_scatter(third_part, 'ctx', scatter_dimension=0, tiled=True)  186 us
    reduce_scatter x1, waiting for transfers between devices, reduce_grads(): lax.psum_scatter(first_part, 'ctx', scatter_dimension=0, tiled=True)  148 us
    unnamed x24, waiting for transfers between devices  141 us
    all_gather x1, waiting for transfers between devices, gather_params(): lax.all_gather(piece_four, 'dp', axis=1, tiled=True)  91.1 us
    all_gather x1, waiting for transfers between devices, gather_params(): lax.all_gather(piece_three, 'dp', axis=1, tiled=True)  63.8 us
    all_gather x1, waiting for transfers between devices, gather_params(): lax.all_gather(piece_one, 'dp', axis=1, tiled=True)  55.4 us
    reduce_scatter x1, waiting for transfers between devices, local(): lax.psum_scatter(join_heads(dvalue_heads), 'ctx', scatter_dimension=0, ti...  51.4 us
  transfers between devices with their start and end apart: 19, of which 17 were waited for; matrix products, arithmetic and copies ran while one was open for 14% of the time, Pallas kernels for 0%

commit v1 on v0

--- a/solution.py
+++ b/solution.py
@@ -18,6 +18,17 @@
 masked_score = -1e30
 
 
+def ring_gather(array, axis, dim):
+    ways = lax.axis_size(axis)
+    pieces = [array]
+    for far in range(1, ways):
+        pieces.append(
+            lax.ppermute(pieces[far - 1], axis, [(d, (d - 1) % ways) for d in range(ways)])
+        )
+    line = jnp.concatenate(pieces, axis=dim)
+    return jnp.roll(line, lax.axis_index(axis) * array.shape[dim], axis=dim)
+
+
 def layer_norm(values):
     center = jnp.mean(values, axis=-1, keepdims=True)
     shifted = values - center
@@ -78,7 +89,7 @@
         lax.all_gather(piece_one, "dp", axis=1, tiled=True),
         lax.all_gather(piece_two, "dp", axis=1, tiled=True),
         lax.all_gather(piece_three, "dp", axis=1, tiled=True),
-        lax.all_gather(piece_four, "dp", axis=1, tiled=True),
+        ring_gather(piece_four, "dp", 1),
         lax.all_gather(piece_five, "dp", axis=1, tiled=True),
     )
 

time: 1600 us -> 1540 us (0.963)
  waiting for transfers between devices: 1090 us -> 1040 us
  local copies, waits for them, and re-layouts: 113 us -> 75.8 us
  other arithmetic: 38.1 us -> 73.7 us
    ppermute x0 -> x3, waiting for transfers between devices: none -> 132 us  [ring_gather(): lax.ppermute(pieces[far - 1], axis, [(d, (d - 1) % ways) for d in range(w...]
    all_gather x1 -> x0, waiting for transfers between devices: 91.1 us -> none  [gather_params(): lax.all_gather(piece_four, 'dp', axis=1, tiled=True)]
    all_gather x1, waiting for transfers between devices: 63.8 us -> 23.7 us  [gather_params(): lax.all_gather(piece_three, 'dp', axis=1, tiled=True)]
    concatenate x0 -> x1, other arithmetic: none -> 37.9 us  [ring_gather(): return jnp.roll(line, lax.axis_index(axis) * array.shape[dim], axis=dim)]
    all_gather x1, waiting for transfers between devices: 27.4 us -> 0.01 us  [gather_keys(): lax.all_gather(value_rows, 'ctx', axis=0, tiled=True)]
    all_gather x1, waiting for transfers between devices: 26 us -> 0.02 us  [gather_keys(): lax.all_gather(key_rows, 'ctx', axis=0, tiled=True)]
    dynamic_update_slice x17, local copies, waits for them, and re-layouts: 22.1 us -> 0.63 us  [local(): lax.map(head_forward, (heads_query, heads_key, heads_value))]
    unnamed x132 -> x118, local copies, waits for them, and re-layouts: 41 us -> 38.2 us
  transfers between devices with their start and end apart: 19 -> 21, of which waited for: 17 -> 16; matrix products, arithmetic and copies ran while one was open for 14% -> 15% of each run, Pallas kernels for 0% -> 0%
where the time goes in v1:
time: 1540 us; the launch traced here: 1530 us
  waiting for transfers between devices  1040 us (68%)
  matrix products  233 us (15%)
  blocking collectives  83 us (5%)
  local copies, waits for them, and re-layouts  75.8 us (5%)
  other arithmetic  73.7 us (5%)
  between operations  17 us (1%)
    reduce_scatter x1, waiting for transfers between devices, reduce_grads(): lax.psum_scatter(fourth_part, 'ctx', scatter_dimension=0, tiled=True)  197 us
    reduce_scatter x1, waiting for transfers between devices, reduce_grads(): lax.psum_scatter(third_part, 'ctx', scatter_dimension=0, tiled=True)  186 us
    reduce_scatter x1, waiting for transfers between devices, reduce_grads(): lax.psum_scatter(first_part, 'ctx', scatter_dimension=0, tiled=True)  148 us
    unnamed x23, waiting for transfers between devices  144 us
    ppermute x3, waiting for transfers between devices, ring_gather(): lax.ppermute(pieces[far - 1], axis, [(d, (d - 1) % ways) for d in range(w...  132 us
    all_gather x1, waiting for transfers between devices, gather_params(): lax.all_gather(piece_one, 'dp', axis=1, tiled=True)  55.4 us
    reduce_scatter x1, waiting for transfers between devices, local(): lax.psum_scatter(join_heads(dvalue_heads), 'ctx', scatter_dimension=0, ti...  51.3 us
    unnamed x2, blocking collectives  45.7 us
  transfers between devices with their start and end apart: 21, of which 16 were waited for; matrix products, arithmetic and copies ran while one was open for 15% of the time, Pallas kernels for 0%

profile of v1, /device:TPU:0, one launch (start us, length us, event | category | flops | bytes accessed | tf_op | source)
XLA Modules:
  0.0 1529.6 jit_solution(17099568616590615897)
XLA Ops:
  9.1 31.8 %all-gather.12.cloned.1.call-done = bf16[1088,816]{1,0:T(8,128)(2,1)} async-done(((bf16[136,816]{1,0:T(8,128)(2,1)}), bf16[1088,816]{1,0:T(8,128)(2,1)}) %all-gather.12.cloned.1.call-update) | async-done | bytes 1775632 | tf_op jit(solution)/shard_map/all_gather | solution.py:82
  40.9 4.0 copy.90
  46.9 12.8 all-gather
  59.8 8.8 all-gather.1
  69.6 55.4 %all-gather.14.cloned.1.call-done = bf16[1088,3264]{0,1:T(8,128)(2,1)} async-done(((bf16[1088,816]{0,1:T(8,128)(2,1)}), bf16[1088,3264]{0,1:T(8,128)(2,1)}) %all-gather.14.cloned.1.call-update) | async-done | bytes 7102480 | tf_op jit(solution)/shard_map/all_gather | solution.py:89
  125.0 5.4 fusion.83
  132.5 29.9 %all-gather.26.cloned.1.call-done = bf16[8,544,272]{1,2,0:T(8,128)(2,1)} async-done(((bf16[1,544,272]{1,2,0:T(8,128)(2,1)}), bf16[8,544,272]{1,2,0:T(8,128)(2,1)}) %all-gather.26.cloned.1.call-update) | async-done | bytes 2367504 | tf_op jit(solution)/shard_map/all_gather | solution.py:85
  164.8 3.1 reshape.198
  170.2 51.5 %collective-permute-done = bf16[4352,272]{0,1:T(8,128)(2,1)} collective-permute-done((bf16[4352,272]{0,1:T(8,128)(2,1)}, bf16[4352,272]{0,1:T(8,128)(2,1)}, u32[]{:S(2)}, u32[]{:S(2)}) %collective-permute-start) | collective-permute-done | bytes 2367520 | tf_op jit(solution)/shard_map/ppermute | solution.py:26
  221.7 3.3 collective-permute-start.1
  225.0 15.8 %all_gather.48 = bf16[1088,272]{1,0:T(8,128)(2,1)S(1)} all-gather(bf16[136,272]{1,0:T(8,128)(2,1)S(1)} %convert_element_type.74), channel_id=1, replica_groups=mesh['dp'=4,'ctx'=8] {'ctx'}, dimensions={0}, use_global_device_ids=true | all-gather | bytes 665856 | tf_op jit(solution)/shard_map/all_gather | solution.py:83
  242.0 38.5 %collective-permute-done.1 = bf16[4352,272]{0,1:T(8,128)(2,1)} collective-permute-done((bf16[4352,272]{0,1:T(8,128)(2,1)}, bf16[4352,272]{0,1:T(8,128)(2,1)}, u32[]{:S(2)}, u32[]{:S(2)}) %collective-permute-start.1) | collective-permute-done | bytes 2367520 | tf_op jit(solution)/shard_map/ppermute | solution.py:26
  280.5 3.4 collective-permute-start.2
  285.1 5.1 copy.96
  290.5 42.5 %collective-permute-done.2 = bf16[4352,272]{0,1:T(8,128)(2,1)} collective-permute-done((bf16[4352,272]{0,1:T(8,128)(2,1)}, bf16[4352,272]{0,1:T(8,128)(2,1)}, u32[]{:S(2)}, u32[]{:S(2)}) %collective-permute-start.2) | collective-permute-done | bytes 2367520 | tf_op jit(solution)/shard_map/ppermute | solution.py:26
  333.0 37.9 %fusion.50 = bf16[4352,1088]{0,1:T(8,128)(2,1)} fusion(s32[]{:T(128)S(6)} %select_n.24, bf16[4352,272]{0,1:T(8,128)(2,1)S(1)} %copy-done.4, bf16[4352,272]{0,1:T(8,128)(2,1)} %collective-permute-done, bf16[4352,272]{0,1:T(8,128)(2,1)} %collective-permute-done.1, bf16[4352,272]{0,1:T(8,128)(2,1)} %collective-permute-done.2), kind=kLoop, calls=%fused_computation.69 | loop fusion | flops 75759616 | bytes 18939908 | tf_op jit(solution)/shard_map/jit(_roll_dynamic)/concatenate | solution.py:29
  371.2 5.2 copy.92
  376.4 5.2 copy.93
  381.7 48.4 %while.28 = (s32[]{:T(128)}, bf16[17,128,64]{1,2,0:T(8,128)(2,1)S(1)}, f32[17,128]{1,0:T(8,128)S(1)}, bf16[17,128,64]{2,1,0:T(8,128)(2,1)S(1)}, bf16[17,1024,64]...) while((s32[]{:T(128)}, ...), condition=%wide.region_5.6_spmd.clone, body=%wide.region_2.5_spmd.clone.sunk | while | flops 34611072 | bytes 2157681 | solution.py:198
  430.9 2.6 fusion.94
  433.7 23.7 %all-gather.24.cloned.1.call-done = bf16[1088,4352]{0,1:T(8,128)(2,1)} async-done(((bf16[1088,1088]{0,1:T(8,128)(2,1)}), bf16[1088,4352]{0,1:T(8,128)(2,1)}) %all-gather.24.cloned.1.call-update) | async-done | bytes 9469968 | tf_op jit(solution)/shard_map/all_gather | solution.py:91
  457.4 7.3 convolution_add_fusion
  464.8 7.5 fusion.95
  472.4 4.3 multiply_reduce_fusion
  478.5 122.2 %while.29 = (s32[]{:T(128)}, f32[17,128,64]{1,2,0:T(8,128)}, f32[17,1024,64]{1,2,0:T(8,128)}, f32[17,1024,64]{1,2,0:T(8,128)}, bf16[17,128,64]{2,1,0:T(8,128)(2,...) while((s32[]{:T(128)}, f32[17,128,64]{1,2,0:T(8,128)}, ...), condition=%wide.region_12.14_spmd.clone, body=%wide.region_10.13_spmd.clone.sunk | while | flops 85098368 | bytes 3944593 | solution.py:255
  601.4 3.0 fusion.77
  606.1 9.7 fusion.76
  617.7 35.7 %reduce-scatter.20.cloned.1.call-done = f32[128,1088]{0,1:T(8,128)} async-done(((f32[1024,1088]{0,1:T(8,128)}), f32[128,1088]{0,1:T(8,128)}) %reduce-scatter.20.cloned.1.call-update) | async-done | bytes 557072 | tf_op jit(solution)/shard_map/reduce_scatter | solution.py:261
  655.1 51.3 %reduce-scatter.22.cloned.1.call-done = f32[128,1088]{0,1:T(8,128)} async-done(((f32[1024,1088]{0,1:T(8,128)}), f32[128,1088]{0,1:T(8,128)}) %reduce-scatter.22.cloned.1.call-update) | async-done | bytes 557072 | tf_op jit(solution)/shard_map/reduce_scatter | solution.py:262
  709.2 8.4 fusion.73
  717.7 9.6 fusion.67
  727.3 37.8 %reduce-scatter.36.cloned.1.call-done = f32[136,1088]{1,0:T(8,128)} async-done(((f32[1088,1088]{1,0:T(8,128)}), f32[136,1088]{1,0:T(8,128)}) %reduce-scatter.36.cloned.1.call-update) | async-done | bytes 591888
  767.6 197.2 %reduce-scatter.28.cloned.1.call-done = f32[544,1088]{1,0:T(8,128)} async-done(((f32[4352,1088]{1,0:T(8,128)}), f32[544,1088]{1,0:T(8,128)}) %reduce-scatter.28.cloned.1.call-update) | async-done | bytes 2367504 | tf_op jit(solution)/shard_map/reduce_scatter | solution.py:102
  964.9 147.8 %reduce-scatter.24.cloned.1.call-done = f32[136,3264]{1,0:T(8,128)} async-done(((f32[1088,3264]{1,0:T(8,128)}), f32[136,3264]{1,0:T(8,128)}) %reduce-scatter.24.cloned.1.call-update) | async-done | bytes 1775632 | tf_op jit(solution)/shard_map/reduce_scatter | solution.py:99
  1112.7 3.4 copy.108
  1116.2 186.2 %reduce-scatter.26.cloned.1.call-done = f32[136,4352]{1,0:T(8,128)} async-done(((f32[1088,4352]{1,0:T(8,128)}), f32[136,4352]{1,0:T(8,128)}) %reduce-scatter.26.cloned.1.call-update) | async-done | bytes 2367504 | tf_op jit(solution)/shard_map/reduce_scatter | solution.py:101
  1302.4 4.9 copy.112
  1323.9 7.4 fusion.57
  1331.4 7.1 multiply_reduce_fusion.1
  1340.2 2.9 concatenate.16
  1343.2 27.9 %all-reduce.2 = f32[1088,12]{0,1:T(8,128)} all-reduce(f32[1088,12]{0,1:T(8,128)} %concatenate.16), channel_id=12, replica_groups=mesh['dp'=4,'ctx'=8] {'ctx'}, use_global_device_ids=true, to_apply=%region_34.36.clone | all-reduce | flops 13056 | bytes 104448
  1372.5 17.8 %all-reduce.3 = f32[136,12]{0,1:T(8,128)} all-reduce(f32[136,12]{0,1:T(8,128)} %constant_dynamic-slice_fusion.2), channel_id=13, replica_groups=mesh['dp'=4,'ctx'=8] {'dp'}, use_global_device_ids=true, to_apply=%region_35.37.clone | all-reduce | flops 1632 | bytes 13056
  1398.0 13.9 all-reduce.6.cloned.1.call-done
  1411.8 3.9 multiply_subtract_fusion
  1422.8 37.7 %reduce-scatter.30.cloned.1.call-done = f32[816,136]{1,0:T(8,128)} async-done(((f32[3264,136]{1,0:T(8,128)}), f32[816,136]{1,0:T(8,128)}) %reduce-scatter.30.cloned.1.call-update) | async-done | bytes 443920
  1461.9 2.7 multiply_subtract_fusion.2
  1464.6 53.6 %reduce-scatter.34.cloned.1.call-done = f32[1088,136]{1,0:T(8,128)} async-done(((f32[4352,136]{1,0:T(8,128)}), f32[1088,136]{1,0:T(8,128)}) %reduce-scatter.34.cloned.1.call-update) | async-done | bytes 591888
  1519.7 2.9 multiply_subtract_fusion.1
  (452 shorter events, 233.5 us)
Async XLA Ops:
  7.2 33.7 %all-gather.12.cloned.1.call-start = ((), (), s32[]{:S(2)}) async-start(), calls=%async_computation.9 | async-start | bytes 2193408 | tf_op jit(solution)/shard_map/all_gather | solution.py:82
  9.0 36.0 %copy-start.13 = (f32[544,272]{0,1:T(8,128)S(1)}, f32[544,272]{0,1:T(8,128)}, u32[]{:S(2)}) copy-start(f32[544,272]{0,1:T(8,128)} %param.30) | copy-start | bytes 1775620
  9.0 116.0 %all-gather.14.cloned.1.call-start = ((), (), s32[]{:S(2)}) async-start(), calls=%async_computation.10 | async-start | bytes 9400320 | tf_op jit(solution)/shard_map/all_gather | solution.py:89
  44.9 23.7 %copy-start = (f32[1,128,1088]{1,2,0:T(8,128)S(1)}, f32[1,128,1088]{1,2,0:T(8,128)}, u32[]{:S(2)}) copy-start(f32[1,128,1088]{1,2,0:T(8,128)} %param.24) | copy-start | bytes 1671172
  44.9 117.5 %all-gather.26.cloned.1.call-start = ((), (), s32[]{:S(2)}) async-start(), calls=%async_computation.21 | async-start | bytes 3133440 | tf_op jit(solution)/shard_map/all_gather | solution.py:85
  45.8 239.3 %all-gather.22.cloned.1.call-start = ((), (), s32[]{:S(2)}) async-start(), calls=%async_computation.14 | async-start | bytes 2820096 | tf_op jit(solution)/shard_map/all_gather | solution.py:84
  46.8 324.4 %all-gather.16.cloned.1.call-start = ((), (), s32[]{:S(2)}) async-start(), calls=%async_computation.11 | async-start | bytes 2506752 | tf_op jit(solution)/shard_map/all_gather | solution.py:116
  68.6 56.4 %copy-start.33 = (f32[12,1088]{1,0:T(8,128)}, f32[12,1088]{1,0:T(8,128)S(1)}, u32[]{:S(2)}) copy-start(f32[12,1088]{1,0:T(8,128)S(1)} %reshape.199) | copy-start | bytes 156676
  69.4 61.0 %copy-start.30 = (f32[1088]{0:T(1024)}, f32[1088]{0:T(1024)S(1)}, u32[]{:S(2)}) copy-start(f32[1088]{0:T(1024)S(1)} %get-tuple-element.324) | copy-start | bytes 13060
  69.4 61.0 %copy-start.35 = (f32[1088]{0:T(1024)}, f32[1088]{0:T(1024)S(1)}, u32[]{:S(2)}) copy-start(f32[1088]{0:T(1024)S(1)} %get-tuple-element.323) | copy-start | bytes 13060
  69.6 60.9 %copy-start.40 = (f32[128]{0:T(128)}, f32[128]{0:T(128)S(1)}, u32[]{:S(2)}) copy-start(f32[128]{0:T(128)S(1)} %add_rsqrt_fusion.1) | copy-start | bytes 1540
  131.2 245.2 %all-gather.18.cloned.1.call-start = ((), (), s32[]{:S(2)}) async-start(), calls=%async_computation.12 | async-start | bytes 2506752 | tf_op jit(solution)/shard_map/all_gather | solution.py:117
  132.5 297.7 %all-gather.20.cloned.1.call-start = ((), (), s32[]{:S(2)}) async-start(), calls=%async_computation.13 | async-start | bytes 3133440 | tf_op jit(solution)/shard_map/all_gather | solution.py:90
  164.7 60.3 %copy-start.25 = (f32[136,272]{1,0:T(8,128)S(1)}, f32[136,272]{1,0:T(8,128)}, u32[]{:S(2)}) copy-start(f32[136,272]{1,0:T(8,128)} %param.28) | copy-start | bytes 443908
  167.8 116.0 %copy-start.44 = (s32[8,2]{0,1:T(2,128)S(1)}, s32[8,2]{0,1:T(2,128)}, u32[]{:S(2)}) copy-start(s32[8,2]{0,1:T(2,128)} %param.26) | copy-start | bytes 196
  167.8 53.9 %collective-permute-start = (bf16[4352,272]{0,1:T(8,128)(2,1)}, bf16[4352,272]{0,1:T(8,128)(2,1)}, u32[]{:S(2)}, u32[]{:S(2)}) collective-permute-start(bf16[4352,272]{0,1:T(8,128)(2,1)} %reshape.198), channel_id=1, source_target_pairs={{0,24},{8,0},{16,8},{24,16},{1,25},{9,1},{17,9},{25,17},{2,26},{10... | collective-permute-start | bytes 7102472 | tf_op jit(solution)/shard_map/ppermute | solution.py:26
  221.7 58.7 %collective-permute-start.1 = (bf16[4352,272]{0,1:T(8,128)(2,1)}, bf16[4352,272]{0,1:T(8,128)(2,1)}, u32[]{:S(2)}, u32[]{:S(2)}) collective-permute-start(bf16[4352,272]{0,1:T(8,128)(2,1)} %collective-permute-done), channel_id=1, source_target_pairs={{0,24},{8,0},{16,8},{24,16},{1,25},{9,1},{17,9},{25,17},{2,26},{10... | collective-permute-start | bytes 7102472 | tf_op jit(solution)/shard_map/ppermute | solution.py:26
  242.0 215.5 %all-gather.24.cloned.1.call-start = ((), (), s32[]{:S(2)}) async-start(), calls=%async_computation.15 | async-start | bytes 12533760 | tf_op jit(solution)/shard_map/all_gather | solution.py:91
  280.5 52.5 %collective-permute-start.2 = (bf16[4352,272]{0,1:T(8,128)(2,1)}, bf16[4352,272]{0,1:T(8,128)(2,1)}, u32[]{:S(2)}, u32[]{:S(2)}) collective-permute-start(bf16[4352,272]{0,1:T(8,128)(2,1)} %collective-permute-done.1), channel_id=1, source_target_pairs={{0,24},{8,0},{16,8},{24,16},{1,25},{9,1},{17,9},{25,17},{2,26},{10... | collective-permute-start | bytes 7102472 | tf_op jit(solution)/shard_map/ppermute | solution.py:26
  290.2 42.7 %copy-start.4 = (bf16[4352,272]{0,1:T(8,128)(2,1)S(1)}, bf16[4352,272]{0,1:T(8,128)(2,1)}, u32[]{:S(2)}) copy-start(bf16[4352,272]{0,1:T(8,128)(2,1)} %reshape.198) | copy-start | bytes 7102468
  290.3 80.6 %copy-start.20 = (bf16[128,1088]{0,1:T(8,128)(2,1)S(1)}, bf16[128,1088]{0,1:T(8,128)(2,1)}, u32[]{:S(2)}) copy-start(bf16[128,1088]{0,1:T(8,128)(2,1)} %get-tuple-element.387) | copy-start | bytes 835588
  290.3 363.0 %reduce-scatter.20.cloned.1.call-start = ((), (), s32[]{:S(2)}) async-start(), calls=%async_computation.16 | async-start | bytes 5013504 | tf_op jit(solution)/shard_map/reduce_scatter | solution.py:261
  381.7 49.2 %copy-start.38 = (f32[1088]{0:T(1024)S(1)}, f32[1088]{0:T(1024)}, u32[]{:S(2)}) copy-start(f32[1088]{0:T(1024)} %get-tuple-element.320) | copy-start | bytes 13060
  430.9 26.5 %copy-start.29 = (f32[1088]{0:T(1024)S(1)}, f32[1088]{0:T(1024)}, u32[]{:S(2)}) copy-start(f32[1088]{0:T(1024)} %get-tuple-element.317) | copy-start | bytes 13060
  430.9 26.5 %copy-start.34 = (f32[1088]{0:T(1024)S(1)}, f32[1088]{0:T(1024)}, u32[]{:S(2)}) copy-start(f32[1088]{0:T(1024)} %get-tuple-element.319) | copy-start | bytes 13060
  457.4 14.9 slice-start
  477.1 124.3 %copy-start.5 = (f32[128,1088]{0,1:T(8,128)}, f32[128,1088]{0,1:T(8,128)S(1)}, u32[]{:S(2)}) copy-start(f32[128,1088]{0,1:T(8,128)S(1)} %get-tuple-element.383) | copy-start | bytes 1671172
  600.8 105.6 %reduce-scatter.22.cloned.1.call-start = ((), (), s32[]{:S(2)}) async-start(), calls=%async_computation.17 | async-start | bytes 5013504 | tf_op jit(solution)/shard_map/reduce_scatter | solution.py:262
  601.3 163.8 %reduce-scatter.36.cloned.1.call-start = ((), (), s32[]{:S(2)}) async-start(), calls=%async_computation.26 | async-start | bytes 5640192
  604.5 360.3 %reduce-scatter.28.cloned.1.call-start = ((), (), s32[]{:S(2)}) async-start(), calls=%async_computation.20 | async-start | bytes 22560768 | tf_op jit(solution)/shard_map/reduce_scatter | solution.py:102
  615.7 93.4 %copy-start.31 = (f32[1088]{0:T(1024)S(1)}, f32[1088]{0:T(1024)}, u32[]{:S(2)}) copy-start(f32[1088]{0:T(1024)} %copy-done.30) | copy-start | bytes 13060
  615.8 93.4 %copy-start.36 = (f32[1088]{0:T(1024)S(1)}, f32[1088]{0:T(1024)}, u32[]{:S(2)}) copy-start(f32[1088]{0:T(1024)} %copy-done.35) | copy-start | bytes 13060
  615.8 93.4 %copy-start.41 = (f32[128]{0:T(128)S(1)}, f32[128]{0:T(128)}, u32[]{:S(2)}) copy-start(f32[128]{0:T(128)} %copy-done.40) | copy-start | bytes 1540
  615.8 496.9 %reduce-scatter.24.cloned.1.call-start = ((), (), s32[]{:S(2)}) async-start(), calls=%async_computation.18 | async-start | bytes 16293888 | tf_op jit(solution)/shard_map/reduce_scatter | solution.py:99
  717.6 584.8 %reduce-scatter.26.cloned.1.call-start = ((), (), s32[]{:S(2)}) async-start(), calls=%async_computation.19 | async-start | bytes 21307392 | tf_op jit(solution)/shard_map/reduce_scatter | solution.py:101
  727.3 667.4 %reduce-scatter.32.cloned.1.call-start = ((), (), s32[]{:S(2)}) async-start(), calls=%async_computation.23 | async-start | bytes 1392640
  767.6 644.2 %all-reduce.6.cloned.1.call-start = ((), (), s32[]{:S(2)}) async-start(), calls=%async_computation.25 | async-start | bytes 5013504
  964.8 495.6 %reduce-scatter.30.cloned.1.call-start = ((), (), s32[]{:S(2)}) async-start(), calls=%async_computation.22 | async-start | bytes 4177920
  1116.1 402.0 %reduce-scatter.34.cloned.1.call-start = ((), (), s32[]{:S(2)}) async-start(), calls=%async_computation.24 | async-start | bytes 5570560
  1331.4 61.6 %copy-start.6 = (f32[128,1088]{0,1:T(8,128)S(1)}, f32[128,1088]{0,1:T(8,128)}, u32[]{:S(2)}) copy-start(f32[128,1088]{0,1:T(8,128)} %copy-done.5) | copy-start | bytes 1671172
  1338.4 57.4 %copy-start.26 = (f32[136,272]{1,0:T(8,128)S(1)}, f32[136,272]{1,0:T(8,128)}, u32[]{:S(2)}) copy-start(f32[136,272]{1,0:T(8,128)} %param.28) | copy-start | bytes 443908
  1338.4 73.4 %copy-start.9 = (f32[544,272]{1,0:T(8,128)S(1)}, f32[544,272]{1,0:T(8,128)}, u32[]{:S(2)}) copy-start(f32[544,272]{1,0:T(8,128)} %copy.103) | copy-start | bytes 1775620
  1338.4 73.4 %copy-start.10 = (f32[544,272]{1,0:T(8,128)S(1)}, f32[544,272]{1,0:T(8,128)}, u32[]{:S(2)}) copy-start(f32[544,272]{1,0:T(8,128)} %copy.100) | copy-start | bytes 1775620
  1395.8 19.8 %copy-start.27 = (f32[136,272]{1,0:T(8,128)}, f32[136,272]{1,0:T(8,128)S(1)}, u32[]{:S(2)}) copy-start(f32[136,272]{1,0:T(8,128)S(1)} %copy.111) | copy-start | bytes 443908
  1420.4 41.4 %copy-start.18 = (f32[136,816]{1,0:T(8,128)S(1)}, f32[136,816]{1,0:T(8,128)}, u32[]{:S(2)}) copy-start(f32[136,816]{1,0:T(8,128)} %param.27) | copy-start | bytes 1331716
  1461.8 57.9 %copy-start.17 = (f32[136,816]{1,0:T(8,128)}, f32[136,816]{1,0:T(8,128)S(1)}, u32[]{:S(2)}) copy-start(f32[136,816]{1,0:T(8,128)S(1)} %copy.109) | copy-start | bytes 1331716
  1461.8 57.9 %copy-start.15 = (f32[136,1088]{1,0:T(8,128)S(1)}, f32[136,1088]{1,0:T(8,128)}, u32[]{:S(2)}) copy-start(f32[136,1088]{1,0:T(8,128)} %param.29) | copy-start | bytes 1775620
  1461.8 57.9 %copy-start.28 = (f32[136,1088]{1,0:T(8,128)S(1)}, f32[136,1088]{1,0:T(8,128)}, u32[]{:S(2)}) copy-start(f32[136,1088]{1,0:T(8,128)} %param.34) | copy-start | bytes 1775620
  (23 other events, 137.0 us)
Sparse Core Ops, SparseCore 0:
  10.2 30.6 all-gather.11
  45.0 79.9 all-gather.13
  127.2 35.0 all-gather.25
  164.5 31.7 all-gather.21
  198.3 31.4 all-gather.15
  231.8 31.3 all-gather.17
  265.6 88.7 all-gather.19
  356.3 101.1 all-gather.23
  600.9 52.3 reduce-scatter.19
  655.5 50.8 reduce-scatter.21
  708.7 56.3 reduce-scatter.35
  767.3 197.4 reduce-scatter.27
  967.1 145.5 reduce-scatter.23
  1114.9 187.4 reduce-scatter.25
  1305.2 26.8 reduce-scatter.31
  1335.2 76.5 all-reduce.5
  1414.7 45.6 reduce-scatter.29
  1463.3 54.7 reduce-scatter.33
